TPU v7x, 512 devices: a whole 4x8x8 slice. The times are simulated.
512 devices in a mesh: terms: 32 (over y_hi, z), rows: 4 (over y_lo, core), cols: 4 (over x).
Axes of the slice: x: 4, y: 8 (y_hi: 4, y_lo: 2; y = y_hi * 2 + y_lo), z: 8, core: 2. Of those that a mesh axis runs over, the one named last changes fastest.
Arguments:
- wavefunction: bfloat16 [2, 1024, 1024], P(None, 'rows', 'cols'), may hold values from -6 to 6
- energy: float32 [2], replicated, may hold values from 1 to 4
- block_rows: int32 [2], replicated, may hold values from 512 to 1024
- block_cols: int32 [2], replicated, may hold values from 512 to 1024
- left_ops: bfloat16 [128, 1024, 1024], P('terms', 'rows'), may hold values from -0.1875 to 0.1875
- right_ops: bfloat16 [128, 1024, 1024], P('terms', 'cols'), may hold values from -0.1875 to 0.1875
- source: int32 [128], P('terms'), may hold values from 0 to 1
- target: int32 [128], P('terms'), may hold values from 0 to 1
Outputs:
- sigma: bfloat16 [2, 1024, 1024], P(None, 'rows', 'cols')
- residual: bfloat16 [2, 1024, 1024], P(None, 'rows', 'cols')
Inputs may be any that keep to these rules, and one draw needn't show every extreme that they name: source[t] is the sector whose block term t reads. target[t] is the sector to which term t adds. `block_rows`: entries of a sector block beyond its live left or right states are ignored.
All inputs are finite; a program needn't handle non-finite values.
Results may differ from a plain program's by a relative error of at most 0.0044.
The roundings to bfloat16 on the way count: a program that leaves them out, or rounds other values in their place, can miss the bound.
Values may be sent and summed in bfloat16 or wider, within the bound.
A program may use at most 64 MiB of HBM per device.

v0:
```python
import jax
import jax.numpy as jnp
from jax import lax
from jax.sharding import PartitionSpec as P

EPSILON = 1e-06


def in_order(blocks, dim):
    shape = list(blocks.shape[1:])
    shape[dim] *= blocks.shape[0]
    return jnp.moveaxis(blocks, 0, dim).reshape(shape)


def copy_for_each(value, axis):
    copies = jnp.broadcast_to(value, (lax.axis_size(axis), *value.shape))
    return lax.all_to_all(copies, axis, split_axis=0, concat_axis=0, tiled=True)


def gathered_copies(value, axis, dim):
    return in_order(copy_for_each(value, axis), dim)


def split_up(value, dim, peers):
    shape = value.shape
    blocks = value.reshape(*shape[:dim], peers, shape[dim] // peers, *shape[dim + 1 :])
    return jnp.moveaxis(blocks, dim, 0)


def sent_and_summed(value, axis, dim):
    blocks = split_up(value, dim, lax.axis_size(axis))
    arrived = lax.all_to_all(blocks, axis, split_axis=0, concat_axis=0, tiled=True)
    return arrived.sum(axis=0)


def filled_up(lines, peers):
    spare = -len(lines) % peers
    return jnp.pad(lines, [(0, spare)] + [(0, 0)] * (lines.ndim - 1))


def total_of(value, axes):
    lines = value.reshape(-1, value.shape[-1])
    own = sent_and_summed(filled_up(lines, lax.axis_size(axes)), axes, 0)
    whole = gathered_copies(own, axes, 0)
    return whole[: len(lines)].reshape(value.shape)


def over_copies(value, axis):
    everything = copy_for_each(value, axis)
    return jnp.sum(everything, axis=0)


def packed_total(arrays, axis):
    ends = [0]
    for a in arrays:
        ends.append(ends[-1] + a.size)
    subtotal = over_copies(jnp.concatenate([a.ravel() for a in arrays]), axis)
    return tuple((subtotal[b:e].reshape(a.shape) for a, b, e in zip(arrays, ends, ends[1:])))


def per_device(wavefunction, energy, block_rows, block_cols, left_ops, right_ops, source, target):
    sectors, tile_rows, tile_cols = wavefunction.shape
    term_count = left_ops.shape[0]
    row_ids = lax.axis_index("rows") * tile_rows + lax.iota(jnp.int32, tile_rows)
    col_ids = lax.axis_index("cols") * tile_cols + lax.iota(jnp.int32, tile_cols)
    inside = (row_ids[None, :, None] < block_rows[:, None, None]) & (
        col_ids[None, None, :] < block_cols[:, None, None]
    )
    live_psi = jnp.where(inside, wavefunction, jnp.zeros_like(wavefunction))
    sector_ids = lax.iota(jnp.int32, sectors)
    partial_value = jnp.zeros((sectors, tile_rows, tile_cols), jnp.float32)
    panels = gathered_copies(live_psi, "rows", 1)
    product_list = []
    for term_index in range(term_count):
        col_panel = lax.dynamic_index_in_dim(panels, source[term_index], 0, keepdims=False)
        product_list.append(
            jnp.dot(left_ops[term_index], col_panel, preferred_element_type=jnp.float32).astype(
                jnp.bfloat16
            )
        )
    products = jnp.stack(product_list)
    additions = jnp.einsum(
        "txl,tml->txm",
        gathered_copies(products, "cols", 2),
        right_ops,
        preferred_element_type=jnp.float32,
    )
    for term_index in range(term_count):
        hit = (sector_ids == target[term_index])[:, None, None]
        partial_value = partial_value + jnp.where(hit, additions[term_index][None], 0.0)
    live_f = live_psi.astype(jnp.float32)
    summed = total_of(partial_value, "terms")
    full_sigma = jnp.where(inside, summed + energy[:, None, None] * live_f, 0.0)
    numerator, denominator = packed_total(
        (jnp.sum(live_f * full_sigma), jnp.sum(live_f * live_f)), ("rows", "cols")
    )
    rayleigh = numerator / (denominator + EPSILON)
    residual = full_sigma - rayleigh * live_f
    return (full_sigma.astype(jnp.bfloat16), residual.astype(jnp.bfloat16))


def solution(mesh):
    in_specs = (
        P(None, "rows", "cols"),
        P(),
        P(),
        P(),
        P("terms", "rows", None),
        P("terms", "cols", None),
        P("terms"),
        P("terms"),
    )
    out_specs = (P(None, "rows", "cols"), P(None, "rows", "cols"))
    return jax.shard_map(
        per_device, mesh=mesh, in_specs=in_specs, out_specs=out_specs, check_vma=False
    )
```

profile of v0, /device:TPU:1, one launch (start us, length us, event | category | flops | bytes accessed | tf_op | source)
XLA Modules:
  0.0 133.9 jit_solution(2646475192078335884)
XLA Ops:
  0.6 0.0 copy-start
  0.6 0.0 copy-start.2
  0.7 0.9 broadcast_compare_fusion
  1.6 1.1 and_select_fusion.1
  2.7 1.0 broadcast_in_dim.117
  3.7 10.3 %all-to-all-start = ((bf16[4,2,256,256]{3,2,1,0:T(8,128)(2,1)}), bf16[4,2,256,256]{3,2,1,0:T(8,128)(2,1)S(1)}, u32[]{:S(2)}, u32[]{:S(2)}) async-start(bf16[4,2,256,256]{3,2,1,0:T(8,128)(2,1)} %broadcast_in_dim.117), calls=%async_computation | async-start | bytes 2097152 | tf_op jit(solution)/shard_map/all_to_all | solution.py:17
  14.0 0.0 copy-done.2
  14.0 0.7 fusion.32
  22.3 5.2 %all-to-all-done = bf16[4,2,256,256]{3,2,1,0:T(8,128)(2,1)S(1)} async-done(((bf16[4,2,256,256]{3,2,1,0:T(8,128)(2,1)}), bf16[4,2,256,256]{3,2,1,0:T(8,128)(2,1)S(1)}, u32[]{:S(2)}, u32[]{:S(2)}) %all-to-all-start) | async-done | bytes 1048608 | tf_op jit(solution)/shard_map/all_to_all | solution.py:17
  27.5 0.0 copy-start.5
  27.5 0.1 copy.18
  27.6 1.5 %copy-done.5 = bf16[4,256,1024]{2,1,0:T(8,128)(2,1)S(1)} copy-done((bf16[4,256,1024]{2,1,0:T(8,128)(2,1)S(1)}, bf16[4,256,1024]{2,1,0:T(8,128)(2,1)}, u32[]{:S(2)}) %copy-start.5) | copy-done | bytes 2097176
  29.1 0.3 fusion
  29.5 0.4 fusion.1
  29.8 0.4 fusion.2
  30.2 0.4 fusion.3
  30.5 0.1 pad_maximum_fusion
  30.6 0.2 copy.19
  30.8 1.5 %broadcast_in_dim.118 = bf16[4,4,256,256]{3,2,1,0:T(8,128)(2,1)} broadcast(bf16[4,256,256]{2,1,0:T(8,128)(2,1)S(1)} %copy.19), dimensions={1,2,3} | broadcast | bytes 2621440 | tf_op jit(solution)/shard_map/broadcast_in_dim | solution.py:16
  32.3 0.0 copy-start.3
  32.3 4.6 %all-to-all-start.1 = ((bf16[4,4,256,256]{3,2,1,0:T(8,128)(2,1)}), bf16[4,4,256,256]{3,2,1,0:T(8,128)(2,1)}, u32[]{:S(2)}, u32[]{:S(2)}) async-start(bf16[4,4,256,256]{3,2,1,0:T(8,128)(2,1)} %broadcast_in_dim.118), calls=%async_computation.1 | async-start | bytes 4194304 | tf_op jit(solution)/shard_map/all_to_all | solution.py:17
  36.9 0.0 copy-done.3
  36.9 0.6 fusion.31
  37.5 0.6 iota_compare_fusion.3
  38.2 0.1 broadcast_in_dim.113
  38.3 0.1 broadcast_in_dim.114
  38.4 0.6 iota_compare_fusion.2
  39.0 0.1 broadcast_in_dim.123
  39.1 0.1 broadcast_in_dim.124
  39.2 0.6 iota_compare_fusion.1
  39.8 0.1 broadcast_in_dim.129
  39.9 0.1 broadcast_in_dim.130
  40.0 0.6 iota_compare_fusion
  40.6 0.1 broadcast_in_dim.135
  40.7 0.1 broadcast_in_dim.136
  40.7 21.7 %all-to-all-done.1 = bf16[4,4,256,256]{3,2,1,0:T(8,128)(2,1)} async-done(((bf16[4,4,256,256]{3,2,1,0:T(8,128)(2,1)}), bf16[4,4,256,256]{3,2,1,0:T(8,128)(2,1)}, u32[]{:S(2)}, u32[]{:S(2)}) %all-to-all-start.1) | async-done | bytes 2097184 | tf_op jit(solution)/shard_map/all_to_all | solution.py:17
  62.4 1.9 %copy.25 = bf16[4,4,32,8,256]{4,3,0,2,1:T(8,128)(2,1)S(1)} copy(bf16[4,4,32,8,256]{4,3,2,1,0:T(8,128)(2,1)} %bitcast.44) | data formatting | bytes 4194304 | tf_op jit(solution)/shard_map/reshape | solution.py:12
  64.3 0.0 copy-done
  64.3 0.7 fusion.33
  65.0 0.1 slice_bitcast_fusion.3
  65.3 0.2 select_add_fusion
  65.5 0.0 copy-start.1
  65.5 0.0 copy-start.4
  65.5 25.1 %all_to_all.26 = f32[32,16,256]{2,1,0:T(8,128)S(1)} all-to-all(f32[32,16,256]{2,1,0:T(8,128)S(1)} %select_add_fusion), channel_id=1, replica_groups=mesh['terms'=32,'rows'=4,'cols'=4] {'terms'}, dimensions={0} | all-to-all | bytes 1048576 | tf_op jit(solution)/shard_map/all_to_all | solution.py:32
  90.7 0.1 broadcast_in_dim.141
  90.8 25.1 %all_to_all.27 = f32[32,16,256]{2,1,0:T(8,128)S(1)} all-to-all(f32[32,16,256]{2,1,0:T(8,128)S(1)} %broadcast_in_dim.141), channel_id=1, replica_groups=mesh['terms'=32,'rows'=4,'cols'=4] {'terms'}, dimensions={0} | all-to-all | bytes 1048576 | tf_op jit(solution)/shard_map/all_to_all | solution.py:17
  115.8 0.0 copy-done.1
  115.8 0.0 copy-done.4
  115.9 0.9 fusion.5
  116.8 1.4 %pad_maximum_fusion.1 = f32[2]{0:T(128)S(1)} fusion(f32[1]{0:T(128)} %bitcast.38, f32[1]{0:T(128)} %bitcast.37), kind=kLoop, calls=%fused_computation.50 | loop fusion | flops 2 | bytes 16 | tf_op jit(solution)/shard_map/concatenate | solution.py:57
  118.1 12.8 %all_to_all.28 = f32[16,1,2]{2,1,0:T(1,128)S(1)} all-to-all(f32[16,1,2]{2,1,0:T(1,128)S(1)} %broadcast_in_dim.143), channel_id=1, replica_groups=mesh['terms'=32,'rows'=4,'cols'=4] {'rows','cols'}, dimensions={0} | all-to-all | bytes 256 | tf_op jit(solution)/shard_map/all_to_all | solution.py:17
  130.9 0.6 fusion.30
  132.8 1.0 fusion.8
  (9 shorter events, 0.2 us)
Async XLA Ops:
  0.6 63.7 %copy-start = (bf16[4,256,1024]{2,1,0:T(8,128)(2,1)S(1)}, bf16[4,256,1024]{2,1,0:T(8,128)(2,1)}, u32[]{:S(2)}) copy-start(bf16[4,256,1024]{2,1,0:T(8,128)(2,1)} %param.13) | copy-start | bytes 6291460
  0.6 13.4 %copy-start.2 = (s32[4]{0:T(128)S(1)}, s32[4]{0:T(128)}, u32[]{:S(2)}) copy-start(s32[4]{0:T(128)} %param.14) | copy-start | bytes 52
  3.7 23.8 %all-to-all-start = ((bf16[4,2,256,256]{3,2,1,0:T(8,128)(2,1)}), bf16[4,2,256,256]{3,2,1,0:T(8,128)(2,1)S(1)}, u32[]{:S(2)}, u32[]{:S(2)}) async-start(bf16[4,2,256,256]{3,2,1,0:T(8,128)(2,1)} %broadcast_in_dim.117), calls=%async_computation | async-start | bytes 2097152 | tf_op jit(solution)/shard_map/all_to_all | solution.py:17
  27.5 1.6 %copy-start.5 = (bf16[4,256,1024]{2,1,0:T(8,128)(2,1)S(1)}, bf16[4,256,1024]{2,1,0:T(8,128)(2,1)}, u32[]{:S(2)}) copy-start(bf16[4,256,1024]{2,1,0:T(8,128)(2,1)} %param.12) | copy-start | bytes 6291460
  32.3 4.6 %copy-start.3 = (s32[4]{0:T(128)S(1)}, s32[4]{0:T(128)}, u32[]{:S(2)}) copy-start(s32[4]{0:T(128)} %param.15) | copy-start | bytes 52
  32.3 30.1 %all-to-all-start.1 = ((bf16[4,4,256,256]{3,2,1,0:T(8,128)(2,1)}), bf16[4,4,256,256]{3,2,1,0:T(8,128)(2,1)}, u32[]{:S(2)}, u32[]{:S(2)}) async-start(bf16[4,4,256,256]{3,2,1,0:T(8,128)(2,1)} %broadcast_in_dim.118), calls=%async_computation.1 | async-start | bytes 4194304 | tf_op jit(solution)/shard_map/all_to_all | solution.py:17
  65.5 50.3 %copy-start.1 = (bf16[2,256,256]{2,1,0:T(8,128)(2,1)S(1)}, bf16[2,256,256]{2,1,0:T(8,128)(2,1)}, u32[]{:S(2)}) copy-start(bf16[2,256,256]{2,1,0:T(8,128)(2,1)} %param.8) | copy-start | bytes 786436
  65.5 50.3 %copy-start.4 = (f32[2]{0:T(128)S(1)}, f32[2]{0:T(128)}, u32[]{:S(2)}) copy-start(f32[2]{0:T(128)} %param.9) | copy-start | bytes 28
where the time goes:
time: 134 us
  blocking collectives  63 us (47%)
  waiting for transfers between devices  26.8 us (20%)
  starting transfers between devices  14.9 us (11%)
  between operations  9.83 us (7%)
  local copies, waits for them, and re-layouts  9.02 us (7%)
  other arithmetic  8.18 us (6%)
  matrix products  2.15 us (2%)
    all_to_all x2, blocking collectives, copy_for_each(): return lax.all_to_all(copies, axis, split_axis=0, concat_axis=0, tiled=True)  37.9 us
    all_to_all x2, waiting for transfers between devices, copy_for_each(): return lax.all_to_all(copies, axis, split_axis=0, concat_axis=0, tiled=True)  26.8 us
    all_to_all x1, blocking collectives, sent_and_summed(): lax.all_to_all(blocks, axis, split_axis=0, concat_axis=0, tiled=True)  25.1 us
    all_to_all x2, starting transfers between devices, copy_for_each(): return lax.all_to_all(copies, axis, split_axis=0, concat_axis=0, tiled=True)  14.9 us
  transfers between devices with their start and end apart: 2, of which 2 were waited for; matrix products, arithmetic and copies ran while one was open for 3% of the time, Pallas kernels for 0%

commit v1 on v0

v1 whole, which is shorter than its diff:
```python
import functools

import jax
import jax.numpy as jnp
from jax import lax
from jax.experimental import pallas as pl
from jax.experimental.pallas import tpu as pltpu
from jax.sharding import PartitionSpec as P

MESH = pl.DeviceIdType.MESH
EPSILON = 1e-06
F32 = jnp.float32
BF16 = jnp.bfloat16
N_SEMS = 96


class Copies:
    def __init__(self, send_sems, recv_sems):
        self.send_sems, self.recv_sems, self.used, self.open = send_sems, recv_sems, 0, []

    def send(self, src, dst, device):
        at = self.used
        self.used += 1
        copy = pltpu.make_async_remote_copy(
            src, dst, self.send_sems.at[at], self.recv_sems.at[at], device_id=device, device_id_type=MESH
        )
        copy.start()
        self.open.append(copy)
        return copy

    def finish(self):
        for copy in self.open:
            copy.wait_send()


def kernel(
    source, target, block_rows, block_cols, energy, psi, left, right,
    sigma, residual,
    psi0, psi1, psi2, psi3, lbuf, rbuf, adds, part, part_b, zbuf, ybuf, summed, own,
    tile1, tile2, tile3, tile4, local_sems, send_sems, recv_sems,
):
    t, r, x = lax.axis_index("terms"), lax.axis_index("rows"), lax.axis_index("cols")
    yhi, z, ylo, core = t // 8, t % 8, r // 2, r % 2
    parity = z % 2

    def at_y(dy):
        y = (yhi * 2 + ylo + dy + 8) % 8
        return {"terms": (y // 2) * 8 + z, "rows": (y % 2) * 2 + core}

    def at_z(dz):
        return {"terms": yhi * 8 + (z + dz + 8) % 8}

    def at_yhi(d):
        return {"terms": ((yhi + d + 4) % 4) * 8 + z}

    def at_x(dx):
        return {"cols": (x + dx + 4) % 4}

    def at_r(d):
        return {"rows": (r + d) % 4}

    partner = {"rows": ylo * 2 + 1 - core}
    z_steps = (4, 3, -3, 2, -2, 1, -1)
    y_steps = (2, 1, -1)
    x_steps = (1, -1, 2)

    barrier = pltpu.get_barrier_semaphore()
    friends = [partner, at_y(1), at_y(-1)]
    friends += [{"rows": (1 - ylo) * 2 + 1 - core}]
    friends += [at_x(d) for d in x_steps] + [at_z(d) for d in z_steps] + [at_yhi(d) for d in y_steps]
    for friend in friends:
        pl.semaphore_signal(barrier, inc=1, device_id=friend, device_id_type=MESH)

    psis = {0: psi0, 1: psi1, 2: psi2, 3: psi3}
    mine = pl.multiple_of(r * 256, 256)
    theirs = pl.multiple_of(((1 - ylo) * 2 + core) * 256, 256)
    native = pltpu.make_async_copy(psi, psi0.at[:, pl.ds(mine, 256), :], local_sems.at[0])
    native.start()
    load_l = pltpu.make_async_copy(left, lbuf, local_sems.at[1])
    load_l.start()
    load_r = pltpu.make_async_copy(right, rbuf, local_sems.at[2])
    load_r.start()
    pl.semaphore_wait(barrier, len(friends))

    copies = Copies(send_sems, recv_sems)
    send = copies.send

    def unit(k, sector, base, half=None):
        if half is None:
            return psis[k].at[sector, pl.ds(base, 256), :]
        return psis[k].at[sector, pl.ds(pl.multiple_of(base + 128 * half, 128), 128), :]

    a_in = {}
    a_in[3] = send(psi.at[parity], unit(3, parity, mine), at_x(1))
    a_in[1] = send(psi.at[parity], unit(1, parity, mine), at_x(-1))
    y_in = [send(psi.at[0], unit(0, 0, mine), at_y(1)), send(psi.at[1], unit(0, 1, mine), at_y(-1))]
    a_in[2] = send(psi.at[parity], unit(2, parity, mine), at_x(2))
    arrivals = {0: [], 1: [], 2: [], 3: []}
    arrivals[0].append(send(psi, psi0.at[:, pl.ds(mine, 256), :], partner))

    def share(k, ref):
        arrivals[k].append(send(ref, ref, partner))

    b_in, c_in = {}, {}

    def pass_on(k):
        a_in[k].wait_recv()
        b_in[k], c_in[k] = [], []
        for half, way in ((0, 1), (1, -1)):
            piece = unit(k, parity, mine, half)
            c_in[k].append(send(piece, piece, at_y(way)))
            b_in[k].append(send(piece, piece, at_z(way)))
        share(k, unit(k, parity, mine))

    d_in = {}

    def turn(k):
        d_in[k] = []
        for half, way in ((0, 1), (1, -1)):
            c_in[k][half].wait_recv()
            piece = unit(k, parity, theirs, half)
            d_in[k].append(send(piece, piece, at_z(way)))
            share(k, piece)

    def take_b(k):
        for half in (0, 1):
            b_in[k][half].wait_recv()
            share(k, unit(k, 1 - parity, mine, half))

    def take_d(k):
        for half in (0, 1):
            d_in[k][half].wait_recv()
            share(k, unit(k, 1 - parity, theirs, half))

    def settle(k):
        for copy in arrivals[k]:
            copy.wait_recv()

    def mask_left():
        load_l.wait()
        columns = lax.broadcasted_iota(jnp.int32, (256, 1024), 1)

        def one(i, carry):
            lbuf[i] = jnp.where(columns < block_rows[source[i]], lbuf[i], jnp.zeros((), BF16))
            return carry

        lax.fori_loop(0, 4, one, 0)

    def compute(k, first):
        start = pl.multiple_of(((x + k) % 4) * 256, 256)
        columns = lax.broadcasted_iota(jnp.int32, (256, 256), 1) + start

        def one(i, carry):
            sector = source[i]
            product = jnp.dot(lbuf[i], psis[k][sector], preferred_element_type=F32)
            product = jnp.where(columns < block_cols[sector], product, 0.0).astype(BF16)
            added = lax.dot_general(
                product, rbuf[i, :, pl.ds(start, 256)], (((1,), (1,)), ((), ())), preferred_element_type=F32
            )
            adds[i] = added if first else adds[i] + added
            return carry

        lax.fori_loop(0, 4, one, 0)

    mask_left()
    pass_on(1)
    pass_on(3)
    for s in (0, 1):
        y_in[s].wait_recv()
        share(0, unit(0, s, theirs))
    turn(1)
    take_b(1)
    pass_on(2)
    turn(3)
    take_b(3)
    native.wait()
    settle(0)
    load_r.wait()
    compute(0, True)
    turn(2)
    take_d(1)
    take_b(2)
    settle(1)
    compute(1, False)
    take_d(3)
    settle(3)
    compute(3, False)
    take_d(2)
    settle(2)
    compute(2, False)

    rows = lax.broadcasted_iota(jnp.int32, (256, 256), 0) + r * 256
    columns = lax.broadcasted_iota(jnp.int32, (256, 256), 1) + x * 256
    numerator = jnp.zeros((8, 256), F32)
    denominator = jnp.zeros((8, 256), F32)
    for s in (0, 1):
        block = jnp.where(target[0] == s, adds[0], 0.0)
        for i in (1, 2, 3):
            block = block + jnp.where(target[i] == s, adds[i], 0.0)
        part[pl.ds(s * 256, 256), :] = block
        part_b[pl.ds(s * 256, 256), :] = block.astype(BF16)
    z_in = []
    for d in z_steps:
        there = pl.multiple_of(((z + d + 8) % 8) * 64, 64)
        z_in.append(send(part_b.at[pl.ds(there, 64), :], zbuf.at[z], at_z(d)))
    for s in (0, 1):
        inside = (rows < block_rows[s]) & (columns < block_cols[s])
        live = jnp.where(inside, psi0[s, pl.ds(mine, 256), :].astype(F32), 0.0)
        own[s] = live
        square = jnp.sum((live * live).reshape(32, 8, 256), axis=0) * (1.0 / 32)
        block = part[pl.ds(s * 256, 256), :]
        numerator += jnp.sum((live * block).reshape(32, 8, 256), axis=0) + energy[s] * square
        denominator += square

    def exchange(value, tiles, here, moves):
        tiles[here] = value
        got = [send(tiles.at[here], tiles.at[here], device) for device in moves]

        def total():
            for copy in got:
                copy.wait_recv()
            whole = tiles[0]
            for i in range(1, tiles.shape[0]):
                whole = whole + tiles[i]
            return whole

        return total

    sums = jnp.concatenate([numerator, denominator], axis=0)
    sums = sums[:, :128] + sums[:, 128:]
    sums = exchange(sums, tile1, r, [at_r(d) for d in (1, 2, 3)])()
    sums_later = exchange(sums, tile2, z, [at_z(d) for d in z_steps])

    for copy in z_in:
        copy.wait_recv()
    here = pl.multiple_of(z * 64, 64)
    total = part[pl.ds(here, 64), :]
    for d in z_steps:
        total = total + zbuf[(z + d + 8) % 8].astype(F32)
    ybuf[yhi] = total.astype(BF16)
    y_got = [send(ybuf.at[yhi], ybuf.at[yhi], at_yhi(d)) for d in y_steps]
    sums_later = exchange(sums_later(), tile3, yhi, [at_yhi(d) for d in y_steps])
    for copy in y_got:
        copy.wait_recv()
    total = ybuf[0].astype(F32)
    for i in (1, 2, 3):
        total = total + ybuf[i].astype(F32)
    summed[pl.ds(here, 64), :] = total.astype(BF16)
    chunk = summed.at[pl.ds(here, 64), :]
    last = [send(chunk, chunk, at_z(d)) for d in z_steps]
    sums = exchange(sums_later(), tile4, x, [at_x(d) for d in x_steps])()
    rayleigh = jnp.sum(sums[:8]) / (jnp.sum(sums[8:]) + EPSILON)
    for copy in last:
        copy.wait_recv()
    for s in (0, 1):
        inside = (rows < block_rows[s]) & (columns < block_cols[s])
        live = own[s]
        full = jnp.where(inside, summed[pl.ds(s * 256, 256), :].astype(F32) + energy[s] * live, 0.0)
        sigma[s] = full.astype(BF16)
        residual[s] = (full - rayleigh * live).astype(BF16)
    copies.finish()


def per_device(wavefunction, energy, block_rows, block_cols, left_ops, right_ops, source, target):
    smem = pl.BlockSpec(memory_space=pltpu.SMEM)
    anyw = pl.BlockSpec(memory_space=pl.ANY)
    vmem = pl.BlockSpec(memory_space=pltpu.VMEM)
    block = jax.ShapeDtypeStruct((2, 256, 256), BF16)
    return pl.pallas_call(
        kernel,
        out_shape=(block, block),
        in_specs=[smem] * 5 + [anyw] * 3,
        out_specs=(vmem, vmem),
        scratch_shapes=[pltpu.VMEM((2, 1024, 256), BF16)] * 4
        + [
            pltpu.VMEM((4, 256, 1024), BF16),
            pltpu.VMEM((4, 256, 1024), BF16),
            pltpu.VMEM((4, 256, 256), F32),
            pltpu.VMEM((512, 256), F32),
            pltpu.VMEM((512, 256), BF16),
            pltpu.VMEM((8, 64, 256), BF16),
            pltpu.VMEM((4, 64, 256), BF16),
            pltpu.VMEM((512, 256), BF16),
            pltpu.VMEM((2, 256, 256), F32),
            pltpu.VMEM((4, 16, 128), F32),
            pltpu.VMEM((8, 16, 128), F32),
            pltpu.VMEM((4, 16, 128), F32),
            pltpu.VMEM((4, 16, 128), F32),
            pltpu.SemaphoreType.DMA((3,)),
            pltpu.SemaphoreType.DMA((N_SEMS,)),
            pltpu.SemaphoreType.DMA((N_SEMS,)),
        ],
        compiler_params=pltpu.CompilerParams(
            collective_id=0, has_side_effects=True, vmem_limit_bytes=40 * 1024 * 1024
        ),
        name="sigma_step",
    )(source, target, block_rows, block_cols, energy, wavefunction, left_ops, right_ops)


def solution(mesh):
    in_specs = (
        P(None, "rows", "cols"),
        P(),
        P(),
        P(),
        P("terms", "rows", None),
        P("terms", "cols", None),
        P("terms"),
        P("terms"),
    )
    out_specs = (P(None, "rows", "cols"), P(None, "rows", "cols"))
    return jax.shard_map(per_device, mesh=mesh, in_specs=in_specs, out_specs=out_specs, check_vma=False)
```

time: 134 us -> 70.8 us (0.53)
  blocking collectives: 63 us -> 0 us
  Pallas kernels: 0 us -> 61.1 us
  waiting for transfers between devices: 26.8 us -> 0 us
  starting transfers between devices: 14.9 us -> 0 us
  between operations: 9.83 us -> 0.66 us
  other arithmetic: 8.18 us -> 0 us
  matrix products: 2.15 us -> 0 us
    all_to_all x3 -> x0, blocking collectives: 63 us -> none  [the longest x2 37.9 us: copy_for_each(): return lax.all_to_all(copies, axis, split_axis=0, concat_axis=0, tiled=True)]
    pallas_call x0 -> x1, Pallas kernels: none -> 61.1 us  [per_device(): pl.pallas_call(kernel, out_shape=(block, block), in_specs=[smem] * 5 + [a...]
    all_to_all x2 -> x0, waiting for transfers between devices: 26.8 us -> none  [copy_for_each(): return lax.all_to_all(copies, axis, split_axis=0, concat_axis=0, tiled=True)]
    all_to_all x2 -> x0, starting transfers between devices: 14.9 us -> none  [copy_for_each(): return lax.all_to_all(copies, axis, split_axis=0, concat_axis=0, tiled=True)]
    unnamed x12 -> x18, local copies, waits for them, and re-layouts: 1.55 us -> 8.81 us
    broadcast_in_dim x17 -> x0, local copies, waits for them, and re-layouts: 3.47 us -> none  [the longest x4 2.61 us: copy_for_each(): copies = jnp.broadcast_to(value, (lax.axis_size(axis), *value.shape))]
    eq x4 -> x0, other arithmetic: 2.53 us -> none  [per_device(): hit = (sector_ids == target[term_index])[:, None, None]]
    dot_general x5 -> x0, matrix products: 2.15 us -> none  [the longest x4 1.41 us: per_device(): jnp.dot(left_ops[term_index], col_panel, preferred_element_type=jnp.float32)]
  transfers between devices with their start and end apart: 2 -> 0, of which waited for: 2 -> 0; matrix products, arithmetic and copies ran while one was open for 3% -> 0% of each run, Pallas kernels for 0% -> 0%
where the time goes in v1:
time: 70.8 us; the launch traced here: 70.6 us
  Pallas kernels  61.1 us (86%)
  local copies, waits for them, and re-layouts  8.81 us (12%)
    pallas_call x1, Pallas kernels, per_device(): pl.pallas_call(kernel, out_shape=(block, block), in_specs=[smem] * 5 + [a...  61.1 us
    unnamed x18, local copies, waits for them, and re-layouts  8.81 us

profile of v1, /device:TPU:1, one launch (start us, length us, event | category | flops | bytes accessed | tf_op | source)
XLA Modules:
  0.0 70.6 jit_solution(18056825876163446642)
XLA Ops:
  0.6 0.0 copy-start
  0.6 1.6 %copy-done = bf16[4,256,1024]{2,1,0:T(8,128)(2,1)S(1)} copy-done((bf16[4,256,1024]{2,1,0:T(8,128)(2,1)S(1)}, bf16[4,256,1024]{2,1,0:T(8,128)(2,1)}, u32[]{:S(2)}) %copy-start) | copy-done | bytes 2097176
  2.2 0.0 copy-start.1
  2.2 1.6 %copy-done.1 = bf16[4,256,1024]{2,1,0:T(8,128)(2,1)S(1)} copy-done((bf16[4,256,1024]{2,1,0:T(8,128)(2,1)S(1)}, bf16[4,256,1024]{2,1,0:T(8,128)(2,1)}, u32[]{:S(2)}) %copy-start.1) | copy-done | bytes 2097176
  3.8 0.0 copy-start.2
  3.8 0.9 %copy-done.2 = bf16[2,256,256]{2,1,0:T(8,128)(2,1)S(1)} copy-done((bf16[2,256,256]{2,1,0:T(8,128)(2,1)S(1)}, bf16[2,256,256]{2,1,0:T(8,128)(2,1)}, u32[]{:S(2)}) %copy-start.2) | copy-done | bytes 262168
  4.8 0.0 copy-start.3
  4.8 0.7 copy-done.3
  5.4 0.0 copy-start.4
  5.4 0.7 copy-done.4
  6.1 0.0 copy-start.5
  6.1 0.7 copy-done.5
  6.7 0.0 copy-start.6
  6.7 0.7 copy-done.6
  7.4 0.0 copy-start.7
  7.4 0.7 copy-done.7
  8.0 61.1 %sigma_step.1 = (bf16[2,256,256]{2,1,0:T(8,128)(2,1)S(1)}, bf16[2,256,256]{2,1,0:T(8,128)(2,1)S(1)}) custom-call(s32[4]{0:T(128)S(1)} %copy-done.3, s32[4]{0:T(128)S(1)} %copy-done.4, s32[2]{0:T(128)S(1)} %copy-done.5, s32[2]{0:T(128)S(1)} %copy-done.6, f32[2]{0:T(128)S(1)} %copy-done.7, bf16[2,256,256]{2,1,0:T(8,128)(2,1)S(1)} %copy-done.2, ...), custom_call_target="tpu_custom_call" | custom-call | tf_op jit(solution)/shard_map/sigma_step/pallas_call | solution.py:269
  69.2 0.7 copy.12
  69.9 0.7 copy.13
Async XLA Ops:
  0.6 1.6 %copy-start = (bf16[4,256,1024]{2,1,0:T(8,128)(2,1)S(1)}, bf16[4,256,1024]{2,1,0:T(8,128)(2,1)}, u32[]{:S(2)}) copy-start(bf16[4,256,1024]{2,1,0:T(8,128)(2,1)} %left.1) | copy-start | bytes 6291460
  2.2 1.6 %copy-start.1 = (bf16[4,256,1024]{2,1,0:T(8,128)(2,1)S(1)}, bf16[4,256,1024]{2,1,0:T(8,128)(2,1)}, u32[]{:S(2)}) copy-start(bf16[4,256,1024]{2,1,0:T(8,128)(2,1)} %right.1) | copy-start | bytes 6291460
  3.8 0.9 %copy-start.2 = (bf16[2,256,256]{2,1,0:T(8,128)(2,1)S(1)}, bf16[2,256,256]{2,1,0:T(8,128)(2,1)}, u32[]{:S(2)}) copy-start(bf16[2,256,256]{2,1,0:T(8,128)(2,1)} %psi.1) | copy-start | bytes 786436
  4.8 0.7 copy-start.3
  5.4 0.7 copy-start.4
  6.1 0.7 copy-start.5
  6.7 0.7 copy-start.6
  7.4 0.7 copy-start.7

commit v2 on v1

v2 whole, which is shorter than its diff:
```python
import functools

import jax
import jax.numpy as jnp
from jax import lax
from jax.experimental import pallas as pl
from jax.experimental.pallas import tpu as pltpu
from jax.sharding import PartitionSpec as P

MESH = pl.DeviceIdType.MESH
EPSILON = 1e-06
F32 = jnp.float32
BF16 = jnp.bfloat16
N_SEMS = 120
VMEM_LIMIT = 67043328


class Copies:
    def __init__(self, send_sems, recv_sems):
        self.send_sems, self.recv_sems, self.used, self.open = send_sems, recv_sems, 0, []

    def send(self, src, dst, device):
        at = self.used
        self.used += 1
        copy = pltpu.make_async_remote_copy(
            src, dst, self.send_sems.at[at], self.recv_sems.at[at], device_id=device, device_id_type=MESH
        )
        copy.start()
        self.open.append(copy)
        return copy

    def finish(self):
        for copy in self.open:
            copy.wait_send()


def kernel(
    source_in, target_in, rows_in, cols_in, energy_in, psi, left, right,
    sigma, residual,
    source, target, block_rows, block_cols, energy,
    psi0, psi1, psi2, psi3, lbuf, rbuf, adds, part, part_b, zbuf, ybuf, summed, own,
    tile1, tile2, tile3, tile4, local_sems, send_sems, recv_sems, hello,
):
    t, r, x = lax.axis_index("terms"), lax.axis_index("rows"), lax.axis_index("cols")
    yhi, z, ylo, core = t // 8, t % 8, r // 2, r % 2
    parity = z % 2

    def at_y(dy):
        y = (yhi * 2 + ylo + dy + 8) % 8
        return {"terms": (y // 2) * 8 + z, "rows": (y % 2) * 2 + core}

    def at_z(dz):
        return {"terms": yhi * 8 + (z + dz + 8) % 8}

    def at_yhi(d):
        return {"terms": ((yhi + d + 4) % 4) * 8 + z}

    def at_x(dx):
        return {"cols": (x + dx + 4) % 4}

    def at_r(d):
        return {"rows": (r + d) % 4}

    partner = {"rows": ylo * 2 + 1 - core}
    z_steps = (4, 3, -3, 2, -2, 1, -1)
    y_steps = (2, 1, -1)
    x_steps = (1, -1, 2)

    def greet(sem, friends):
        for friend in friends:
            pl.semaphore_signal(sem, inc=1, device_id=friend, device_id_type=MESH)

    line = [at_y(1), at_y(-1), at_z(1), at_z(-1)]
    near = [partner, at_x(1), at_x(-1)] + line
    barrier = pltpu.get_barrier_semaphore()
    greet(barrier, near)

    psis = {0: psi0, 1: psi1, 2: psi2, 3: psi3}
    mine = pl.multiple_of(r * 256, 256)
    theirs = pl.multiple_of(((1 - ylo) * 2 + core) * 256, 256)
    tables = ((source_in, source), (target_in, target), (rows_in, block_rows), (cols_in, block_cols), (energy_in, energy))
    small = [pltpu.make_async_copy(a, b, local_sems.at[3 + i]) for i, (a, b) in enumerate(tables)]
    for copy in small:
        copy.start()
    native = pltpu.make_async_copy(psi, psi0.at[:, pl.ds(mine, 256), :], local_sems.at[0])
    native.start()
    load_l = pltpu.make_async_copy(left, lbuf, local_sems.at[1])
    load_l.start()
    load_r = pltpu.make_async_copy(right, rbuf, local_sems.at[2])
    load_r.start()
    pl.semaphore_wait(barrier, len(near))
    greet(hello.at[0], near)

    copies = Copies(send_sems, recv_sems)
    send = copies.send

    def unit(k, sector, base, half=None):
        if half is None:
            return psis[k].at[sector, pl.ds(base, 256), :]
        return psis[k].at[sector, pl.ds(pl.multiple_of(base + 128 * half, 128), 128), :]

    arrivals = {0: [], 1: [], 2: [], 3: []}
    a_in = {1: [], 2: [], 3: []}
    b_in = {1: [], 2: [], 3: []}
    c_in = {1: [], 2: [], 3: []}
    d_in = {1: [], 2: [], 3: []}
    y_in = {0: [], 1: []}
    for half in (0, 1):
        rows = pl.ds(128 * half, 128)
        a_in[3].append(send(psi.at[parity, rows, :], unit(3, parity, mine, half), at_x(1)))
        a_in[1].append(send(psi.at[parity, rows, :], unit(1, parity, mine, half), at_x(-1)))
        y_in[0].append(send(psi.at[0, rows, :], unit(0, 0, mine, half), at_y(1)))
        y_in[1].append(send(psi.at[1, rows, :], unit(0, 1, mine, half), at_y(-1)))
    arrivals[0].append(send(psi, psi0.at[:, pl.ds(mine, 256), :], partner))

    def share(k, ref):
        arrivals[k].append(send(ref, ref, partner))

    def settle(k):
        for copy in arrivals[k]:
            copy.wait_recv()

    def compute(k, first):
        start = pl.multiple_of(((x + k) % 4) * 256, 256)
        columns = lax.broadcasted_iota(jnp.int32, (256, 256), 1) + start

        def one(i, carry):
            sector = source[i]
            product = jnp.dot(lbuf[i], psis[k][sector], preferred_element_type=F32)
            product = jnp.where(columns < block_cols[sector], product, 0.0).astype(BF16)
            added = lax.dot_general(
                product, rbuf[i, :, pl.ds(start, 256)], (((1,), (1,)), ((), ())), preferred_element_type=F32
            )
            adds[i] = added if first else adds[i] + added
            return carry

        lax.fori_loop(0, 4, one, 0)

    for copy in small:
        copy.wait()
    load_l.wait()
    depth = lax.broadcasted_iota(jnp.int32, (256, 1024), 1)

    def mask_one(i, carry):
        lbuf[i] = jnp.where(depth < block_rows[source[i]], lbuf[i], jnp.zeros((), BF16))
        return carry

    lax.fori_loop(0, 4, mask_one, 0)

    ways = (1, -1)
    for half, k in ((0, 3), (0, 1), (1, 1), (1, 3)):
        a_in[k][half].wait_recv()
        piece = unit(k, parity, mine, half)
        if (half, k) in ((0, 3), (1, 1)):
            a_in[2].append(send(piece, unit(2, parity, mine, half), at_x(ways[half])))
        b_in[k].append(send(piece, piece, at_z(ways[half])))
    for k in (1, 3):
        share(k, unit(k, parity, mine))
    pl.semaphore_wait(hello.at[0], len(near))
    greet(hello.at[1], line)
    for half in (0, 1):
        for s in (0, 1):
            y_in[s][half].wait_recv()
        piece = unit(0, parity, theirs, half)
        c_in[3].append(send(piece, unit(3, parity, theirs, half), at_x(1)))
        c_in[1].append(send(piece, unit(1, parity, theirs, half), at_x(-1)))
    for s in (0, 1):
        share(0, unit(0, s, theirs))
    for half in (0, 1):
        a_in[2][half].wait_recv()
        piece = unit(2, parity, mine, half)
        c_in[2].append(send(piece, piece, at_y(ways[half])))
        b_in[2].append(send(piece, piece, at_z(ways[half])))
    share(2, unit(2, parity, mine))
    for half, k in ((0, 3), (0, 1), (1, 1), (1, 3)):
        b_in[k][half].wait_recv()
        piece = unit(k, 1 - parity, mine, half)
        d_in[k].append(send(piece, piece, at_y(ways[half])))
    for k in (1, 3):
        share(k, unit(k, 1 - parity, mine))
    pl.semaphore_wait(hello.at[1], len(line))
    greet(hello.at[2], line)
    for half in (0, 1):
        c_in[2][half].wait_recv()
        piece = unit(2, parity, theirs, half)
        d_in[2].append(send(piece, piece, at_z(ways[half])))
    share(2, unit(2, parity, theirs))
    for k in (1, 3):
        for half in (0, 1):
            c_in[k][half].wait_recv()
        share(k, unit(k, parity, theirs))
    for half in (0, 1):
        b_in[2][half].wait_recv()
    share(2, unit(2, 1 - parity, mine))
    native.wait()
    settle(0)
    load_r.wait()
    compute(0, True)
    for k in (1, 3):
        for half in (0, 1):
            d_in[k][half].wait_recv()
        share(k, unit(k, 1 - parity, theirs))
    pl.semaphore_wait(hello.at[2], len(line))
    for half in (0, 1):
        d_in[2][half].wait_recv()
    share(2, unit(2, 1 - parity, theirs))
    settle(1)
    compute(1, False)
    settle(3)
    compute(3, False)
    settle(2)
    compute(2, False)

    rows = lax.broadcasted_iota(jnp.int32, (256, 256), 0) + r * 256
    columns = lax.broadcasted_iota(jnp.int32, (256, 256), 1) + x * 256
    z_in = {0: [], 1: []}
    for s in (0, 1):
        block = jnp.where(target[0] == s, adds[0], 0.0)
        for i in (1, 2, 3):
            block = block + jnp.where(target[i] == s, adds[i], 0.0)
        part[s] = block
        part_b[s] = block.astype(BF16)
        for d in z_steps:
            there = pl.multiple_of(((z + d + 8) % 8) * 32, 32)
            z_in[s].append(send(part_b.at[s, pl.ds(there, 32), :], zbuf.at[s, z], at_z(d)))
    numerator = jnp.zeros((8, 256), F32)
    denominator = jnp.zeros((8, 256), F32)
    for s in (0, 1):
        inside = (rows < block_rows[s]) & (columns < block_cols[s])
        live = jnp.where(inside, psi0[s, pl.ds(mine, 256), :].astype(F32), 0.0)
        own[s] = live
        square = jnp.sum((live * live).reshape(32, 8, 256), axis=0) * (1.0 / 32)
        numerator += jnp.sum((live * part[s]).reshape(32, 8, 256), axis=0) + energy[s] * square
        denominator += square

    def exchange(value, tiles, here, moves):
        tiles[here] = value
        got = [send(tiles.at[here], tiles.at[here], device) for device in moves]

        def total():
            for copy in got:
                copy.wait_recv()
            whole = tiles[0]
            for i in range(1, tiles.shape[0]):
                whole = whole + tiles[i]
            return whole

        return total

    sums = jnp.concatenate([numerator, denominator], axis=0)
    sums = sums[:, :128] + sums[:, 128:]
    later = exchange(sums, tile1, r, [at_r(d) for d in (1, 2, 3)])
    later = exchange(later(), tile2, z, [at_z(d) for d in z_steps])

    here = pl.multiple_of(z * 32, 32)
    y_got = {}
    for s in (0, 1):
        for copy in z_in[s]:
            copy.wait_recv()
        total = part[s, pl.ds(here, 32), :]
        for d in z_steps:
            total = total + zbuf[s, (z + d + 8) % 8].astype(F32)
        ybuf[s, yhi] = total.astype(BF16)
        y_got[s] = [send(ybuf.at[s, yhi], ybuf.at[s, yhi], at_yhi(d)) for d in y_steps]
    later = exchange(later(), tile3, yhi, [at_yhi(d) for d in y_steps])
    last = []
    for s in (0, 1):
        for copy in y_got[s]:
            copy.wait_recv()
        total = ybuf[s, 0].astype(F32)
        for i in (1, 2, 3):
            total = total + ybuf[s, i].astype(F32)
        summed[s, pl.ds(here, 32), :] = total.astype(BF16)
        chunk = summed.at[s, pl.ds(here, 32), :]
        last += [send(chunk, chunk, at_z(d)) for d in z_steps]
    later = exchange(later(), tile4, x, [at_x(d) for d in x_steps])
    sums = later()
    rayleigh = jnp.sum(sums[:8]) / (jnp.sum(sums[8:]) + EPSILON)
    for copy in last:
        copy.wait_recv()
    for s in (0, 1):
        inside = (rows < block_rows[s]) & (columns < block_cols[s])
        live = own[s]
        full = jnp.where(inside, summed[s].astype(F32) + energy[s] * live, 0.0)
        sigma[s] = full.astype(BF16)
        residual[s] = (full - rayleigh * live).astype(BF16)
    copies.finish()


def per_device(wavefunction, energy, block_rows, block_cols, left_ops, right_ops, source, target):
    hbm = pl.BlockSpec(memory_space=pltpu.HBM)
    vmem = pl.BlockSpec(memory_space=pltpu.VMEM)
    block = jax.ShapeDtypeStruct((2, 256, 256), BF16)
    return pl.pallas_call(
        kernel,
        out_shape=(block, block),
        in_specs=[hbm] * 8,
        out_specs=(vmem, vmem),
        scratch_shapes=[pltpu.SMEM((4,), jnp.int32)] * 2
        + [pltpu.SMEM((2,), jnp.int32)] * 2
        + [pltpu.SMEM((2,), F32)]
        + [pltpu.VMEM((2, 1024, 256), BF16)] * 4
        + [
            pltpu.VMEM((4, 256, 1024), BF16),
            pltpu.VMEM((4, 256, 1024), BF16),
            pltpu.VMEM((4, 256, 256), F32),
            pltpu.VMEM((2, 256, 256), F32),
            pltpu.VMEM((2, 256, 256), BF16),
            pltpu.VMEM((2, 8, 32, 256), BF16),
            pltpu.VMEM((2, 4, 32, 256), BF16),
            pltpu.VMEM((2, 256, 256), BF16),
            pltpu.VMEM((2, 256, 256), F32),
            pltpu.VMEM((4, 16, 128), F32),
            pltpu.VMEM((8, 16, 128), F32),
            pltpu.VMEM((4, 16, 128), F32),
            pltpu.VMEM((4, 16, 128), F32),
            pltpu.SemaphoreType.DMA((8,)),
            pltpu.SemaphoreType.DMA((N_SEMS,)),
            pltpu.SemaphoreType.DMA((N_SEMS,)),
            pltpu.SemaphoreType.REGULAR((3,)),
        ],
        compiler_params=pltpu.CompilerParams(
            collective_id=0, has_side_effects=True, vmem_limit_bytes=VMEM_LIMIT
        ),
        name="sigma_step",
    )(source, target, block_rows, block_cols, energy, wavefunction, left_ops, right_ops)


def solution(mesh):
    in_specs = (
        P(None, "rows", "cols"),
        P(),
        P(),
        P(),
        P("terms", "rows", None),
        P("terms", "cols", None),
        P("terms"),
        P("terms"),
    )
    out_specs = (P(None, "rows", "cols"), P(None, "rows", "cols"))
    return jax.shard_map(per_device, mesh=mesh, in_specs=in_specs, out_specs=out_specs, check_vma=False)
```

time: 70.8 us -> 60.8 us (0.86)
  local copies, waits for them, and re-layouts: 8.81 us -> 3.34 us
  Pallas kernels: 61.1 us -> 56.6 us
    unnamed x18 -> x2, local copies, waits for them, and re-layouts: 8.81 us -> 3.34 us
    pallas_call x1, Pallas kernels: 61.1 us -> 56.6 us  [per_device(): pl.pallas_call(kernel, out_shape=(block, block), in_specs=[hbm] * 8, out_...]
where the time goes in v2:
time: 60.8 us; the launch traced here: 60.6 us
  Pallas kernels  56.6 us (93%)
  local copies, waits for them, and re-layouts  3.34 us (5%)
  between operations  0.64 us (1%)
    pallas_call x1, Pallas kernels, per_device(): pl.pallas_call(kernel, out_shape=(block, block), in_specs=[hbm] * 8, out_...  56.6 us
    unnamed x2, local copies, waits for them, and re-layouts  3.34 us

profile of v2, /device:TPU:1, one launch (start us, length us, event | category | flops | bytes accessed | tf_op | source)
XLA Modules:
  0.0 60.6 jit_solution(11459239424946850018)
XLA Ops:
  0.6 56.6 %sigma_step.1 = (bf16[2,256,256]{2,1,0:T(8,128)(2,1)}, bf16[2,256,256]{2,1,0:T(8,128)(2,1)}) custom-call(s32[4]{0:T(128)} %source_in.1, s32[4]{0:T(128)} %target_in.1, s32[2]{0:T(128)} %rows_in.1, s32[2]{0:T(128)} %cols_in.1, f32[2]{0:T(128)} %energy_in.1, bf16[2,256,256]{2,1,0:T(8,128)(2,1)} %psi.1, bf16[4,256,1024]{2,1,0:T(8,128)(2,1)} %left.1, ...), custom_call_target="tpu_custom_call" | custom-call | tf_op jit(solution)/shard_map/sigma_step/pallas_call | solution.py:294
  57.3 1.7 %copy.12 = bf16[2,256,256]{2,1,0:T(8,128)(2,1)} copy(bf16[2,256,256]{2,1,0:T(8,128)(2,1)} %get-tuple-element.4) | data formatting | bytes 524288
  58.9 1.7 %copy.13 = bf16[2,256,256]{2,1,0:T(8,128)(2,1)} copy(bf16[2,256,256]{2,1,0:T(8,128)(2,1)} %get-tuple-element.5) | data formatting | bytes 524288

commit v3 on v2

v3 whole, which is shorter than its diff:
```python
import functools

import jax
import jax.numpy as jnp
from jax import lax
from jax.experimental import pallas as pl
from jax.experimental.pallas import tpu as pltpu
from jax.sharding import PartitionSpec as P

MESH = pl.DeviceIdType.MESH
EPSILON = 1e-06
F32 = jnp.float32
BF16 = jnp.bfloat16
N_SEMS = 152
BATCHES = 4
BATCH_ROWS = 512 // BATCHES
CHUNK = BATCH_ROWS // 8
VMEM_LIMIT = 67043328


class Copies:
    def __init__(self, send_sems, recv_sems):
        self.send_sems, self.recv_sems, self.used, self.open = send_sems, recv_sems, 0, []

    def send(self, src, dst, device):
        at = self.used
        self.used += 1
        copy = pltpu.make_async_remote_copy(
            src, dst, self.send_sems.at[at], self.recv_sems.at[at], device_id=device, device_id_type=MESH
        )
        copy.start()
        self.open.append(copy)
        return copy

    def finish(self):
        for copy in self.open:
            copy.wait_send()


def kernel(
    source_in, target_in, rows_in, cols_in, energy_in, psi, left, right,
    summed, live_out, table,
    source, target, block_rows, block_cols, energy,
    own0, own1, own2, own3, far0, far1, far2, far3, half_products, lbuf, rbuf, adds, part, part_b, zbuf, ybuf,
    tile1, tile2, tile3, tile4, local_sems, send_sems, recv_sems, hello,
):
    t, r, x = lax.axis_index("terms"), lax.axis_index("rows"), lax.axis_index("cols")
    yhi, z, ylo, core = t // 8, t % 8, r // 2, r % 2
    parity = z % 2

    def at_y(dy):
        y = (yhi * 2 + ylo + dy + 8) % 8
        return {"terms": (y // 2) * 8 + z, "rows": (y % 2) * 2 + core}

    def at_z(dz):
        return {"terms": yhi * 8 + (z + dz + 8) % 8}

    def at_yhi(d):
        return {"terms": ((yhi + d + 4) % 4) * 8 + z}

    def at_x(dx):
        return {"cols": (x + dx + 4) % 4}

    def at_r(d):
        return {"rows": (r + d) % 4}

    partner = {"rows": ylo * 2 + 1 - core}
    z_steps = (4, 3, -3, 2, -2, 1, -1)
    y_steps = (2, 1, -1)
    x_steps = (1, -1, 2)

    def greet(sem, friends):
        for friend in friends:
            pl.semaphore_signal(sem, inc=1, device_id=friend, device_id_type=MESH)

    line = [at_y(1), at_y(-1), at_z(1), at_z(-1)]
    near = [partner, at_x(1), at_x(-1)] + line
    barrier = pltpu.get_barrier_semaphore()
    greet(barrier, near)

    owns = {0: own0, 1: own1, 2: own2, 3: own3}
    fars = {0: far0, 1: far1, 2: far2, 3: far3}
    mine = pl.multiple_of(core * 256, 256)
    tables = ((source_in, source), (target_in, target), (rows_in, block_rows), (cols_in, block_cols), (energy_in, energy))
    small = [pltpu.make_async_copy(a, b, local_sems.at[3 + i]) for i, (a, b) in enumerate(tables)]
    native = pltpu.make_async_copy(psi, own0.at[:, pl.ds(mine, 256), :], local_sems.at[0])
    native.start()
    for copy in small:
        copy.start()
    native.wait()
    pl.semaphore_wait(barrier, len(near))

    copies = Copies(send_sems, recv_sems)
    send = copies.send

    def unit(group, k, sector, half=None):
        if half is None:
            return group[k].at[sector, pl.ds(mine, 256), :]
        return group[k].at[sector, pl.ds(pl.multiple_of(mine + 128 * half, 128), 128), :]

    a_in = {1: [], 2: [], 3: []}
    b_in = {1: [], 2: [], 3: []}
    c_in = {1: [], 2: [], 3: []}
    d_in = {1: [], 2: [], 3: []}
    y_in = {0: [], 1: []}
    for half in (0, 1):
        piece = unit(owns, 0, parity, half)
        a_in[3].append(send(piece, unit(owns, 3, parity, half), at_x(1)))
        a_in[1].append(send(piece, unit(owns, 1, parity, half), at_x(-1)))
        y_in[0].append(send(unit(owns, 0, 0, half), unit(fars, 0, 0, half), at_y(1)))
        y_in[1].append(send(unit(owns, 0, 1, half), unit(fars, 0, 1, half), at_y(-1)))
    block = own0.at[:, pl.ds(mine, 256), :]
    own_in = {0: [send(block, block, partner)], 1: [], 2: [], 3: []}
    far_in = {0: [], 1: [], 2: [], 3: []}
    greet(hello.at[0], near)
    load_l = pltpu.make_async_copy(left, lbuf, local_sems.at[1])
    load_l.start()
    load_r = pltpu.make_async_copy(right, rbuf, local_sems.at[2])
    load_r.start()

    def share(arrivals, k, ref):
        arrivals[k].append(send(ref, ref, partner))

    def compute_own(k):
        for copy in own_in[k]:
            copy.wait_recv()
        depth = pl.multiple_of(ylo * 512, 512)

        for i in range(4):
            half_products[k, i] = jnp.dot(
                lbuf[i, :, pl.ds(depth, 512)], owns[k][source[i]], preferred_element_type=F32
            )

    def compute_far(k):
        for copy in far_in[k]:
            copy.wait_recv()
        depth = pl.multiple_of((1 - ylo) * 512, 512)
        start = pl.multiple_of(((x + k) % 4) * 256, 256)
        columns = lax.broadcasted_iota(jnp.int32, (256, 256), 1) + start

        for i in range(4):
            sector = source[i]
            product = half_products[k, i] + jnp.dot(
                lbuf[i, :, pl.ds(depth, 512)], fars[k][sector], preferred_element_type=F32
            )
            product = jnp.where(columns < block_cols[sector], product, 0.0).astype(BF16)
            added = lax.dot_general(
                product, rbuf[i, :, pl.ds(start, 256)], (((1,), (1,)), ((), ())), preferred_element_type=F32
            )
            adds[i] = added if k == 0 else adds[i] + added

    for copy in small:
        copy.wait()
    load_l.wait()
    depth_ids = lax.broadcasted_iota(jnp.int32, (256, 1024), 1)

    def mask_one(i, carry):
        lbuf[i] = jnp.where(depth_ids < block_rows[source[i]], lbuf[i], jnp.zeros((), BF16))
        return carry

    lax.fori_loop(0, 4, mask_one, 0)

    ways = (1, -1)
    for half, k in ((0, 3), (0, 1), (1, 1), (1, 3)):
        a_in[k][half].wait_recv()
        piece = unit(owns, k, parity, half)
        if (half, k) in ((0, 3), (1, 1)):
            a_in[2].append(send(piece, unit(owns, 2, parity, half), at_x(ways[half])))
        b_in[k].append(send(piece, piece, at_z(ways[half])))
    for k in (1, 3):
        share(own_in, k, unit(owns, k, parity))
    pl.semaphore_wait(hello.at[0], len(near))
    greet(hello.at[1], line)
    for half in (0, 1):
        for s in (0, 1):
            y_in[s][half].wait_recv()
        piece = unit(fars, 0, parity, half)
        c_in[3].append(send(piece, unit(fars, 3, parity, half), at_x(1)))
        c_in[1].append(send(piece, unit(fars, 1, parity, half), at_x(-1)))
    for s in (0, 1):
        share(far_in, 0, unit(fars, 0, s))
    for half in (0, 1):
        a_in[2][half].wait_recv()
        piece = unit(owns, 2, parity, half)
        c_in[2].append(send(piece, unit(fars, 2, parity, half), at_y(ways[half])))
        b_in[2].append(send(piece, piece, at_z(ways[half])))
    share(own_in, 2, unit(owns, 2, parity))
    compute_own(0)
    for half, k in ((0, 3), (0, 1), (1, 1), (1, 3)):
        b_in[k][half].wait_recv()
        d_in[k].append(send(unit(owns, k, 1 - parity, half), unit(fars, k, 1 - parity, half), at_y(ways[half])))
    for k in (1, 3):
        share(own_in, k, unit(owns, k, 1 - parity))
    pl.semaphore_wait(hello.at[1], len(line))
    greet(hello.at[2], line)
    for k in (1, 3):
        for half in (0, 1):
            c_in[k][half].wait_recv()
        share(far_in, k, unit(fars, k, parity))
    for half in (0, 1):
        c_in[2][half].wait_recv()
        piece = unit(fars, 2, parity, half)
        d_in[2].append(send(piece, piece, at_z(ways[half])))
    share(far_in, 2, unit(fars, 2, parity))
    for half in (0, 1):
        b_in[2][half].wait_recv()
    share(own_in, 2, unit(owns, 2, 1 - parity))
    load_r.wait()
    compute_far(0)
    compute_own(1)
    for k in (1, 3):
        for half in (0, 1):
            d_in[k][half].wait_recv()
        share(far_in, k, unit(fars, k, 1 - parity))
    compute_own(3)
    pl.semaphore_wait(hello.at[2], len(line))
    for half in (0, 1):
        d_in[2][half].wait_recv()
    share(far_in, 2, unit(fars, 2, 1 - parity))
    compute_own(2)
    compute_far(1)
    compute_far(3)
    compute_far(2)

    rows = lax.broadcasted_iota(jnp.int32, (256, 256), 0) + r * 256
    columns = lax.broadcasted_iota(jnp.int32, (256, 256), 1) + x * 256
    z_in = []
    for b in range(BATCHES):
        s, first = divmod(b * BATCH_ROWS, 256)
        span = slice(first, first + BATCH_ROWS)
        block = jnp.where(target[0] == s, adds[0, span, :], 0.0)
        for i in (1, 2, 3):
            block = block + jnp.where(target[i] == s, adds[i, span, :], 0.0)
        part[b] = block
        part_b[b] = block.astype(BF16)
        z_in.append([])
        for d in z_steps:
            there = pl.multiple_of(((z + d + 8) % 8) * CHUNK, CHUNK)
            z_in[b].append(send(part_b.at[b, pl.ds(there, CHUNK), :], zbuf.at[b, z], at_z(d)))
    numerator = jnp.zeros((8, 256), F32)
    denominator = jnp.zeros((8, 256), F32)
    for s in (0, 1):
        inside = (rows < block_rows[s]) & (columns < block_cols[s])
        live = jnp.where(inside, own0[s, pl.ds(mine, 256), :].astype(F32), 0.0)
        live_out[s] = live.astype(BF16)
        square = jnp.sum((live * live).reshape(32, 8, 256), axis=0) * (1.0 / 32)
        half = BATCHES // 2
        block = part[s * half : (s + 1) * half].reshape(256, 256)
        numerator += jnp.sum((live * block).reshape(32, 8, 256), axis=0) + energy[s] * square
        denominator += square

    def exchange(value, tiles, here, moves):
        tiles[here] = value
        got = [send(tiles.at[here], tiles.at[here], device) for device in moves]

        def total():
            for copy in got:
                copy.wait_recv()
            whole = tiles[0]
            for i in range(1, tiles.shape[0]):
                whole = whole + tiles[i]
            return whole

        return total

    sums = jnp.concatenate([numerator, denominator], axis=0)
    sums = sums[:, :128] + sums[:, 128:]
    later = exchange(sums, tile1, r, [at_r(d) for d in (1, 2, 3)])
    later = exchange(later(), tile2, z, [at_z(d) for d in z_steps])

    here = pl.multiple_of(z * CHUNK, CHUNK)
    chunk_rows = lax.broadcasted_iota(jnp.int32, (CHUNK, 256), 0) + (r * 256 + z * CHUNK)
    chunk_columns = lax.broadcasted_iota(jnp.int32, (CHUNK, 256), 1) + x * 256
    y_got, last = [], []

    def along_y(b):
        for copy in z_in[b]:
            copy.wait_recv()
        total = part[b, pl.ds(here, CHUNK), :]
        for d in z_steps:
            total = total + zbuf[b, (z + d + 8) % 8].astype(F32)
        ybuf[b, yhi] = total.astype(BF16)
        y_got.append([send(ybuf.at[b, yhi], ybuf.at[b, yhi], at_yhi(d)) for d in y_steps])

    def along_z(b):
        for copy in y_got[b]:
            copy.wait_recv()
        s, first = divmod(b * BATCH_ROWS, 256)
        total = ybuf[b, 0].astype(F32)
        for i in (1, 2, 3):
            total = total + ybuf[b, i].astype(F32)
        inside = (chunk_rows + first < block_rows[s]) & (chunk_columns < block_cols[s])
        at = pl.ds(pl.multiple_of(first + z * CHUNK, CHUNK), CHUNK)
        summed[s, at, :] = jnp.where(inside, total, 0.0).astype(BF16)
        chunk = summed.at[s, at, :]
        last.extend([send(chunk, chunk, at_z(d)) for d in z_steps])

    for b in range(BATCHES):
        along_y(b)
    later = exchange(later(), tile3, yhi, [at_yhi(d) for d in y_steps])
    for b in range(BATCHES):
        along_z(b)
    sums = exchange(later(), tile4, x, [at_x(d) for d in x_steps])()
    table[0:1, :] = jnp.full((1, 128), jnp.sum(sums[:8]) / (jnp.sum(sums[8:]) + EPSILON), F32)
    table[1:2, :] = jnp.full((1, 128), energy[0], F32)
    table[2:3, :] = jnp.full((1, 128), energy[1], F32)
    for copy in last:
        copy.wait_recv()
    copies.finish()


def finish_kernel(summed, live_in, table, sigma, residual):
    rayleigh = table[0:1, 0:1]
    for s in (0, 1):
        live = live_in[s].astype(F32)
        full = summed[s].astype(F32) + table[1 + s : 2 + s, 0:1] * live
        sigma[s] = full.astype(BF16)
        residual[s] = (full - rayleigh * live).astype(BF16)


def per_device(wavefunction, energy, block_rows, block_cols, left_ops, right_ops, source, target):
    hbm = pl.BlockSpec(memory_space=pltpu.HBM)
    vmem = pl.BlockSpec(memory_space=pltpu.VMEM)
    block = jax.ShapeDtypeStruct((2, 256, 256), BF16)
    parts = pl.pallas_call(
        kernel,
        out_shape=(block, block, jax.ShapeDtypeStruct((8, 128), F32)),
        in_specs=[hbm] * 8,
        out_specs=(vmem, vmem, vmem),
        scratch_shapes=[pltpu.SMEM((4,), jnp.int32)] * 2
        + [pltpu.SMEM((2,), jnp.int32)] * 2
        + [pltpu.SMEM((2,), F32)]
        + [pltpu.VMEM((2, 512, 256), BF16)] * 8
        + [pltpu.VMEM((4, 4, 256, 256), F32)]
        + [
            pltpu.VMEM((4, 256, 1024), BF16),
            pltpu.VMEM((4, 256, 1024), BF16),
            pltpu.VMEM((4, 256, 256), F32),
            pltpu.VMEM((BATCHES, BATCH_ROWS, 256), F32),
            pltpu.VMEM((BATCHES, BATCH_ROWS, 256), BF16),
            pltpu.VMEM((BATCHES, 8, CHUNK, 256), BF16),
            pltpu.VMEM((BATCHES, 4, CHUNK, 256), BF16),
            pltpu.VMEM((4, 16, 128), F32),
            pltpu.VMEM((8, 16, 128), F32),
            pltpu.VMEM((4, 16, 128), F32),
            pltpu.VMEM((4, 16, 128), F32),
            pltpu.SemaphoreType.DMA((8,)),
            pltpu.SemaphoreType.DMA((N_SEMS,)),
            pltpu.SemaphoreType.DMA((N_SEMS,)),
            pltpu.SemaphoreType.REGULAR((3,)),
        ],
        compiler_params=pltpu.CompilerParams(
            collective_id=0, has_side_effects=True, vmem_limit_bytes=VMEM_LIMIT
        ),
        name="sigma_step",
    )(source, target, block_rows, block_cols, energy, wavefunction, left_ops, right_ops)
    return pl.pallas_call(
        finish_kernel,
        out_shape=(block, block),
        in_specs=[vmem] * 3,
        out_specs=(vmem, vmem),
        name="sigma_and_residual",
    )(*parts)


def solution(mesh):
    in_specs = (
        P(None, "rows", "cols"),
        P(),
        P(),
        P(),
        P("terms", "rows", None),
        P("terms", "cols", None),
        P("terms"),
        P("terms"),
    )
    out_specs = (P(None, "rows", "cols"), P(None, "rows", "cols"))
    return jax.shard_map(per_device, mesh=mesh, in_specs=in_specs, out_specs=out_specs, check_vma=False)
```

time: 60.8 us -> 56.4 us (0.928)
  local copies, waits for them, and re-layouts: 3.34 us -> 0 us
  Pallas kernels: 56.6 us -> 55.4 us
    unnamed x2 -> x0, local copies, waits for them, and re-layouts: 3.34 us -> none
    pallas_call x1 -> x2, Pallas kernels: 56.6 us -> 55.4 us  [the longest x1 53.4 us: per_device(): pl.pallas_call(kernel, out_shape=(block, block, jax.ShapeDtypeStruct((8,...]
where the time goes in v3:
time: 56.4 us; the launch traced here: 56 us
  Pallas kernels  55.4 us (98%)
  between operations  0.64 us (1%)
    pallas_call x1, Pallas kernels, per_device(): pl.pallas_call(kernel, out_shape=(block, block, jax.ShapeDtypeStruct((8,...  53.4 us
    pallas_call x1, Pallas kernels, per_device(): pl.pallas_call(finish_kernel, out_shape=(block, block), in_specs=[vmem] *...  2 us

profile of v3, /device:TPU:1, one launch (start us, length us, event | category | flops | bytes accessed | tf_op | source)
XLA Modules:
  0.0 56.0 jit_solution(15973562882005465705)
XLA Ops:
  0.6 53.4 %sigma_step.1 = (bf16[2,256,256]{2,1,0:T(8,128)(2,1)}, bf16[2,256,256]{2,1,0:T(8,128)(2,1)}, f32[8,128]{1,0:T(8,128)}) custom-call(s32[4]{0:T(128)} %source_in.1, s32[4]{0:T(128)} %target_in.1, s32[2]{0:T(128)} %rows_in.1, s32[2]{0:T(128)} %cols_in.1, f32[2]{0:T(128)} %energy_in.1, bf16[2,256,256]{2,1,0:T(8,128)(2,1)} %psi.1, bf16[4,256,1024]{2,1,0:T(8,128)(2,1)} %left.1, ...), custom_call_target="tpu_custom_call" | custom-call | tf_op jit(solution)/shard_map/sigma_step/pallas_call | solution.py:325
  54.0 2.0 %sigma_and_residual.1 = (bf16[2,256,256]{2,1,0:T(8,128)(2,1)}, bf16[2,256,256]{2,1,0:T(8,128)(2,1)}) custom-call(bf16[2,256,256]{2,1,0:T(8,128)(2,1)} %get-tuple-element.5.summed, bf16[2,256,256]{2,1,0:T(8,128)(2,1)} %get-tuple-element.6.live_in, f32[8,128]{1,0:T(8,128)} %get-tuple-element.7.table), custom_call_target="tpu_custom_call" | custom-call | tf_op jit(solution)/shard_map/sigma_and_residual/pallas_call | solution.py:357

commit v4 on v3

--- a/solution.py
+++ b/solution.py
@@ -11,7 +11,7 @@
 EPSILON = 1e-06
 F32 = jnp.float32
 BF16 = jnp.bfloat16
-N_SEMS = 152
+N_SEMS = 160
 BATCHES = 4
 BATCH_ROWS = 512 // BATCHES
 CHUNK = BATCH_ROWS // 8
@@ -57,6 +57,10 @@
 
     def at_yhi(d):
         return {"terms": ((yhi + d + 4) % 4) * 8 + z}
+
+    def at_corner(way):
+        y = (yhi * 2 + ylo + way + 8) % 8
+        return {"terms": (y // 2) * 8 + (z + way + 8) % 8, "rows": (y % 2) * 2 + core}
 
     def at_x(dx):
         return {"cols": (x + dx + 4) % 4}
@@ -93,25 +97,24 @@
     copies = Copies(send_sems, recv_sems)
     send = copies.send
 
-    def unit(group, k, sector, half=None):
-        if half is None:
-            return group[k].at[sector, pl.ds(mine, 256), :]
-        return group[k].at[sector, pl.ds(pl.multiple_of(mine + 128 * half, 128), 128), :]
+    def unit(group, k, sector, piece=0, pieces=1):
+        size = 256 // pieces
+        return group[k].at[sector, pl.ds(pl.multiple_of(mine + size * piece, size), size), :]
 
     a_in = {1: [], 2: [], 3: []}
     b_in = {1: [], 2: [], 3: []}
     c_in = {1: [], 2: [], 3: []}
     d_in = {1: [], 2: [], 3: []}
     y_in = {0: [], 1: []}
-    for half in (0, 1):
-        piece = unit(owns, 0, parity, half)
-        a_in[3].append(send(piece, unit(owns, 3, parity, half), at_x(1)))
-        a_in[1].append(send(piece, unit(owns, 1, parity, half), at_x(-1)))
-        y_in[0].append(send(unit(owns, 0, 0, half), unit(fars, 0, 0, half), at_y(1)))
-        y_in[1].append(send(unit(owns, 0, 1, half), unit(fars, 0, 1, half), at_y(-1)))
     block = own0.at[:, pl.ds(mine, 256), :]
     own_in = {0: [send(block, block, partner)], 1: [], 2: [], 3: []}
     far_in = {0: [], 1: [], 2: [], 3: []}
+    for q in (0, 1):
+        piece = unit(owns, 0, parity, q, 2)
+        a_in[3].append(send(piece, unit(owns, 3, parity, q, 2), at_x(1)))
+        a_in[1].append(send(piece, unit(owns, 1, parity, q, 2), at_x(-1)))
+        y_in[0].append(send(unit(owns, 0, 0, q, 2), unit(fars, 0, 0, q, 2), at_y(1)))
+        y_in[1].append(send(unit(owns, 0, 1, q, 2), unit(fars, 0, 1, q, 2), at_y(-1)))
     greet(hello.at[0], near)
     load_l = pltpu.make_async_copy(left, lbuf, local_sems.at[1])
     load_l.start()
@@ -160,65 +163,64 @@
 
     lax.fori_loop(0, 4, mask_one, 0)
 
+    compute_own(0)
     ways = (1, -1)
-    for half, k in ((0, 3), (0, 1), (1, 1), (1, 3)):
-        a_in[k][half].wait_recv()
-        piece = unit(owns, k, parity, half)
-        if (half, k) in ((0, 3), (1, 1)):
-            a_in[2].append(send(piece, unit(owns, 2, parity, half), at_x(ways[half])))
-        b_in[k].append(send(piece, piece, at_z(ways[half])))
-    for k in (1, 3):
-        share(own_in, k, unit(owns, k, parity))
+    for q in (0, 1):
+        for k in (1, 3):
+            a_in[k][q].wait_recv()
+            piece = unit(owns, k, parity, q, 2)
+            b_in[k].append(send(piece, piece, at_z(ways[q])))
+            if k == (3, 1)[q]:
+                a_in[2].append(send(piece, unit(owns, 2, parity, q, 2), at_x(ways[q])))
+            share(own_in, k, piece)
     pl.semaphore_wait(hello.at[0], len(near))
     greet(hello.at[1], line)
-    for half in (0, 1):
+    for q in (0, 1):
         for s in (0, 1):
-            y_in[s][half].wait_recv()
-        piece = unit(fars, 0, parity, half)
-        c_in[3].append(send(piece, unit(fars, 3, parity, half), at_x(1)))
-        c_in[1].append(send(piece, unit(fars, 1, parity, half), at_x(-1)))
-    for s in (0, 1):
-        share(far_in, 0, unit(fars, 0, s))
-    for half in (0, 1):
-        a_in[2][half].wait_recv()
-        piece = unit(owns, 2, parity, half)
-        c_in[2].append(send(piece, unit(fars, 2, parity, half), at_y(ways[half])))
-        b_in[2].append(send(piece, piece, at_z(ways[half])))
-    share(own_in, 2, unit(owns, 2, parity))
-    compute_own(0)
-    for half, k in ((0, 3), (0, 1), (1, 1), (1, 3)):
-        b_in[k][half].wait_recv()
-        d_in[k].append(send(unit(owns, k, 1 - parity, half), unit(fars, k, 1 - parity, half), at_y(ways[half])))
-    for k in (1, 3):
-        share(own_in, k, unit(owns, k, 1 - parity))
+            y_in[s][q].wait_recv()
+        piece = unit(fars, 0, parity, q, 2)
+        c_in[1].append(send(piece, unit(fars, 1, parity, q, 2), at_x(-1)))
+        c_in[3].append(send(piece, unit(fars, 3, parity, q, 2), at_x(1)))
+        for s in (0, 1):
+            share(far_in, 0, unit(fars, 0, s, q, 2))
+
+    def corner_rows(k):
+        for q in (0, 1):
+            b_in[k][q].wait_recv()
+            piece, there = unit(owns, k, 1 - parity, q, 2), unit(fars, k, 1 - parity, q, 2)
+            d_in[k].append(send(piece, there, at_y(ways[q])))
+            share(own_in, k, piece)
+
+    def pass_to_partner(arrived, arrivals, group, k, sector):
+        for q in (0, 1):
+            arrived[k][q].wait_recv()
+            share(arrivals, k, unit(group, k, sector, q, 2))
+
+    corner_rows(1)
+    for q in (0, 1):
+        a_in[2][q].wait_recv()
+        piece, there = unit(owns, 2, parity, q, 2), unit(fars, 2, parity, q, 2)
+        b_in[2].append(send(piece, piece, at_z(ways[q])))
+        d_in[2].append(send(piece, there, at_corner(ways[q])))
+        c_in[2].append(send(piece, there, at_y(ways[q])))
+        share(own_in, 2, piece)
+    corner_rows(3)
     pl.semaphore_wait(hello.at[1], len(line))
     greet(hello.at[2], line)
-    for k in (1, 3):
-        for half in (0, 1):
-            c_in[k][half].wait_recv()
-        share(far_in, k, unit(fars, k, parity))
-    for half in (0, 1):
-        c_in[2][half].wait_recv()
-        piece = unit(fars, 2, parity, half)
-        d_in[2].append(send(piece, piece, at_z(ways[half])))
-    share(far_in, 2, unit(fars, 2, parity))
-    for half in (0, 1):
-        b_in[2][half].wait_recv()
-    share(own_in, 2, unit(owns, 2, 1 - parity))
     load_r.wait()
     compute_far(0)
+    pass_to_partner(c_in, far_in, fars, 1, parity)
+    pass_to_partner(d_in, far_in, fars, 1, 1 - parity)
+    pass_to_partner(c_in, far_in, fars, 3, parity)
     compute_own(1)
-    for k in (1, 3):
-        for half in (0, 1):
-            d_in[k][half].wait_recv()
-        share(far_in, k, unit(fars, k, 1 - parity))
+    compute_far(1)
+    pass_to_partner(b_in, own_in, owns, 2, 1 - parity)
+    pass_to_partner(c_in, far_in, fars, 2, parity)
+    pass_to_partner(d_in, far_in, fars, 3, 1 - parity)
+    pass_to_partner(d_in, far_in, fars, 2, 1 - parity)
     compute_own(3)
+    compute_own(2)
     pl.semaphore_wait(hello.at[2], len(line))
-    for half in (0, 1):
-        d_in[2][half].wait_recv()
-    share(far_in, 2, unit(fars, 2, 1 - parity))
-    compute_own(2)
-    compute_far(1)
     compute_far(3)
     compute_far(2)
 

time: 56.4 us -> 55.4 us (0.982)
  Pallas kernels: 55.4 us -> 54.5 us
    pallas_call x1, Pallas kernels: 53.4 us -> 52.5 us  [per_device(): pl.pallas_call(kernel, out_shape=(block, block, jax.ShapeDtypeStruct((8,...]
where the time goes in v4:
time: 55.4 us; the launch traced here: 55.2 us
  Pallas kernels  54.5 us (98%)
  between operations  0.64 us (1%)
    pallas_call x1, Pallas kernels, per_device(): pl.pallas_call(kernel, out_shape=(block, block, jax.ShapeDtypeStruct((8,...  52.5 us
    pallas_call x1, Pallas kernels, per_device(): pl.pallas_call(finish_kernel, out_shape=(block, block), in_specs=[vmem] *...  2 us

profile of v4, /device:TPU:1, one launch (start us, length us, event | category | flops | bytes accessed | tf_op | source)
XLA Modules:
  0.0 55.2 jit_solution(8412787995784903611)
XLA Ops:
  0.6 52.5 %sigma_step.1 = (bf16[2,256,256]{2,1,0:T(8,128)(2,1)}, bf16[2,256,256]{2,1,0:T(8,128)(2,1)}, f32[8,128]{1,0:T(8,128)}) custom-call(s32[4]{0:T(128)} %source_in.1, s32[4]{0:T(128)} %target_in.1, s32[2]{0:T(128)} %rows_in.1, s32[2]{0:T(128)} %cols_in.1, f32[2]{0:T(128)} %energy_in.1, bf16[2,256,256]{2,1,0:T(8,128)(2,1)} %psi.1, bf16[4,256,1024]{2,1,0:T(8,128)(2,1)} %left.1, ...), custom_call_target="tpu_custom_call" | custom-call | tf_op jit(solution)/shard_map/sigma_step/pallas_call | solution.py:327
  53.2 2.0 %sigma_and_residual.1 = (bf16[2,256,256]{2,1,0:T(8,128)(2,1)}, bf16[2,256,256]{2,1,0:T(8,128)(2,1)}) custom-call(bf16[2,256,256]{2,1,0:T(8,128)(2,1)} %get-tuple-element.5.summed, bf16[2,256,256]{2,1,0:T(8,128)(2,1)} %get-tuple-element.6.live_in, f32[8,128]{1,0:T(8,128)} %get-tuple-element.7.table), custom_call_target="tpu_custom_call" | custom-call | tf_op jit(solution)/shard_map/sigma_and_residual/pallas_call | solution.py:359

commit v5 on v4

--- a/solution.py
+++ b/solution.py
@@ -91,6 +91,8 @@
     native.start()
     for copy in small:
         copy.start()
+    load_l = pltpu.make_async_copy(left, lbuf, local_sems.at[1])
+    load_l.start()
     native.wait()
     pl.semaphore_wait(barrier, len(near))
 
@@ -116,8 +118,6 @@
         y_in[0].append(send(unit(owns, 0, 0, q, 2), unit(fars, 0, 0, q, 2), at_y(1)))
         y_in[1].append(send(unit(owns, 0, 1, q, 2), unit(fars, 0, 1, q, 2), at_y(-1)))
     greet(hello.at[0], near)
-    load_l = pltpu.make_async_copy(left, lbuf, local_sems.at[1])
-    load_l.start()
     load_r = pltpu.make_async_copy(right, rbuf, local_sems.at[2])
     load_r.start()
 

time: 55.4 us -> 55.4 us (level)
  no operation moved by 1% of the time
where the time goes in v5:
time: 55.4 us; the launch traced here: 55.2 us
  Pallas kernels  54.5 us (98%)
  between operations  0.64 us (1%)
    pallas_call x1, Pallas kernels, per_device(): pl.pallas_call(kernel, out_shape=(block, block, jax.ShapeDtypeStruct((8,...  52.5 us
    pallas_call x1, Pallas kernels, per_device(): pl.pallas_call(finish_kernel, out_shape=(block, block), in_specs=[vmem] *...  2 us

profile of v5, /device:TPU:1, one launch (start us, length us, event | category | flops | bytes accessed | tf_op | source)
XLA Modules:
  0.0 55.2 jit_solution(9857116014008575293)
XLA Ops:
  0.6 52.5 %sigma_step.1 = (bf16[2,256,256]{2,1,0:T(8,128)(2,1)}, bf16[2,256,256]{2,1,0:T(8,128)(2,1)}, f32[8,128]{1,0:T(8,128)}) custom-call(s32[4]{0:T(128)} %source_in.1, s32[4]{0:T(128)} %target_in.1, s32[2]{0:T(128)} %rows_in.1, s32[2]{0:T(128)} %cols_in.1, f32[2]{0:T(128)} %energy_in.1, bf16[2,256,256]{2,1,0:T(8,128)(2,1)} %psi.1, bf16[4,256,1024]{2,1,0:T(8,128)(2,1)} %left.1, ...), custom_call_target="tpu_custom_call" | custom-call | tf_op jit(solution)/shard_map/sigma_step/pallas_call | solution.py:327
  53.2 2.0 %sigma_and_residual.1 = (bf16[2,256,256]{2,1,0:T(8,128)(2,1)}, bf16[2,256,256]{2,1,0:T(8,128)(2,1)}) custom-call(bf16[2,256,256]{2,1,0:T(8,128)(2,1)} %get-tuple-element.5.summed, bf16[2,256,256]{2,1,0:T(8,128)(2,1)} %get-tuple-element.6.live_in, f32[8,128]{1,0:T(8,128)} %get-tuple-element.7.table), custom_call_target="tpu_custom_call" | custom-call | tf_op jit(solution)/shard_map/sigma_and_residual/pallas_call | solution.py:359
